TPU v7x, 32 devices: a whole 2x2x4 slice. The times are simulated.
32 devices in a mesh: gx: 4 (over y, x), gy: 4 (over z), gz: 2 (over core).
Axes of the slice: x: 2, y: 2, z: 4, core: 2. Of those that a mesh axis runs over, the one named last changes fastest.
Arguments:
- populations: float32 [19, 32, 32, 512], P(None, 'gx', 'gz', 'gy'), may hold values from 0.005 to 0.6, as said below
- link_cell: int32 [4, 2, 4, 1024], P('gx', 'gz', 'gy'), may hold values from 0 to 16383, as said below
- link_dir: int32 [4, 2, 4, 1024], P('gx', 'gz', 'gy'), may hold values from 0 to 18, as said below
- link_slot: int32 [4, 2, 4, 1024], P('gx', 'gz', 'gy'), may hold values from 0 to 127, as said below
- link_arm: float32 [3, 4, 2, 4, 1024], P(None, 'gx', 'gz', 'gy'), may hold values from -6 to 6
- brick_bodies: int32 [4, 2, 4, 128], P('gx', 'gz', 'gy'), may hold values from 0 to 2047, as said below
- body_pos: float32 [3, 2048], P(None, ('gx', 'gy')), may hold values from -1 to 1
- body_quat: float32 [4, 2048], P(None, ('gx', 'gy')), may hold values from -1 to 1, as said below
- body_vel: float32 [3, 2048], P(None, ('gx', 'gy')), may hold values from -0.4 to 0.4
- body_spin: float32 [3, 2048], P(None, ('gx', 'gy')), may hold values from -0.4 to 0.4
- inv_mass: float32 [2048], P(('gx', 'gy')), may hold values from 0.5 to 4
- inv_inertia: float32 [3, 2048], P(None, ('gx', 'gy')), may hold values from 0.2 to 2
Outputs:
- next_populations: float32 [19, 32, 32, 512], P(None, 'gx', 'gz', 'gy')
- body_next: float32 [13, 2048], P(None, ('gx', 'gy'))
Inputs may be any that keep to these rules, and one draw needn't show every extreme that they name: `populations`: every entry is positive, and the density (sum over the 19 directions) at every cell lies between 0.5 and 1.6. `link_cell`: within a brick all entries name different cells. `link_dir`: within a brick the used entries (direction 1 to 18) come first, unused ones have direction 0; some brick uses all 1024 entries in every draw. `link_slot`: unused entries hold 0. `brick_bodies`: each brick lists 128 different bodies; owner k holds bodies k*128 to (k+1)*128 - 1; a brick lists at most 16 bodies of one owner, and exactly 16 of some owner in every brick. `body_quat`: unit quaternions.
All inputs are finite; a program needn't handle non-finite values.
Results may differ from a plain program's by a relative error of at most 0.00013.
Values sent between devices are 32-bit elements; how exact they have to be, the bound alone decides.
A program may use at most 64 MiB of HBM per device.

v0:
```python
import functools

import jax
import jax.numpy as jnp
import numpy as np
from jax import lax
from jax.experimental import pallas as pl
from jax.experimental.pallas import tpu as pltpu
from jax.sharding import PartitionSpec as P

VEL = [
    (0, 0, 0), (1, 0, 0), (-1, 0, 0), (0, 1, 0), (0, -1, 0), (0, 0, 1), (0, 0, -1),
    (1, 1, 0), (-1, -1, 0), (1, -1, 0), (-1, 1, 0), (1, 0, 1), (-1, 0, -1), (1, 0, -1),
    (-1, 0, 1), (0, 1, 1), (0, -1, -1), (0, 1, -1), (0, -1, 1),
]
WT = [1.0 / 3.0] + [1.0 / 18.0] * 6 + [1.0 / 36.0] * 12
OPP = [0, 2, 1, 4, 3, 6, 5, 8, 7, 10, 9, 12, 11, 14, 13, 16, 15, 18, 17]
OMEGA = 1.25
POP_CHUNKS = 2
K1_VMEM = 48 * 1024 * 1024
K2_VMEM = 1024 * 1024
GRAV = 0.02
F32 = jnp.float32
BF16 = jnp.bfloat16


def dirs_of(comp, sign):
    return [d for d in range(19) if VEL[d][comp] == sign]


XD = (dirs_of(0, 1), dirs_of(0, -1))
YD = (dirs_of(1, 1), dirs_of(1, -1))
ZD = (dirs_of(2, 1), dirs_of(2, -1))
XZD = tuple([d for d in XD[s] if VEL[d][2] != 0] for s in range(2))


def split3(v):
    hi = v.astype(BF16).astype(F32)
    rest = v - hi
    mid = rest.astype(BF16).astype(F32)
    return hi, mid, rest - mid


def dot(a, b, ca, cb):
    return lax.dot_general(a, b, (((ca,), (cb,)), ((), ())), preferred_element_type=F32)


def stacked(v):
    return jnp.concatenate(split3(v), 0).astype(BF16)


def unstacked(v):
    k = v.shape[0] // 3
    return v[0:k] + v[k : 2 * k] + v[2 * k : 3 * k]


def kernel(
    sizes,
    pop_h, *rest,
):
    small_h, (nxt, bnext, pop), rest = rest[:11], rest[11:14], rest[14:]
    small, rest = rest[:11], rest[11:]
    step(sizes, pop_h, small_h, pop, *small, nxt, bnext, *rest)


def step(
    sizes, pop_h, small_h,
    pop, lcell, ldir, lslot, larm, bb_ref, bpos, bquat, bvel, bspin, imass, iinert,
    nxt, bnext,
    relaxed, sendx, xin, sendz, zin, sende, ein, sendy, yin, yflat, ycols,
    dmap, wmap, motion_own, motion_all, tiles, force_all, half, half_in,
    hs, hr, ms, mr, fs, fr, cs, cr, ps, ss,
):
    ngx, ngy = sizes
    owners = ngx * ngy
    span_x, span_z, span_y = pop.shape[1:]
    cells = span_x * span_z
    links = lcell.shape[-1]
    body_own = bvel.shape[1]
    slots = bb_ref.shape[-1]
    a, b, e = lax.axis_index("gx"), lax.axis_index("gy"), lax.axis_index("gz")
    me = a * ngy + b
    ap, am = lax.rem(a + 1, ngx), lax.rem(a + ngx - 1, ngx)
    bp, bm = lax.rem(b + 1, ngy), lax.rem(b + ngy - 1, ngy)
    oe = 1 - e

    def dev(x, y, z):
        return {"gx": x, "gy": y, "gz": z}

    def peer_of(offset):
        p = lax.rem(me + offset, owners)
        return p, dev(p // ngy, lax.rem(p, ngy), e)

    unroll = owners <= 16

    def loop(lo, hi, body):
        if unroll:
            for i in range(lo, hi):
                body(i)
        else:
            pl.loop(lo, hi)(body)

    small = (lcell, ldir, lslot, larm, bb_ref, bpos, bquat, bvel, bspin, imass, iinert)
    small_in = [
        pltpu.make_async_copy(src, dst, ss.at[k]) for k, (src, dst) in enumerate(zip(small_h, small))
    ]
    chunk = span_x // POP_CHUNKS
    pop_in = [
        pltpu.make_async_copy(
            pop_h.at[:, pl.ds(k * chunk, chunk)], pop.at[:, pl.ds(k * chunk, chunk)], ps.at[k]
        )
        for k in range(POP_CHUNKS)
    ]
    for k in (7, 8):
        small_in[k].start()
    for c in pop_in:
        c.start()
    for k in (0, 1, 2, 3, 4, 5, 6, 9, 10):
        small_in[k].start()

    barrier = pltpu.get_barrier_semaphore()

    def greet(o):
        pl.semaphore_signal(barrier, inc=1, device_id=peer_of(o)[1], device_id_type=pl.DeviceIdType.MESH)

    loop(1, owners, greet)
    others = [dev(a, b, oe), dev(ap, b, oe), dev(am, b, oe), dev(a, bp, oe), dev(a, bm, oe)]
    for t in others:
        pl.semaphore_signal(barrier, inc=1, device_id=t, device_id_type=pl.DeviceIdType.MESH)

    small_in[7].wait()
    small_in[8].wait()
    motion_own[...] = jnp.concatenate(
        [bvel[...], bspin[...], jnp.zeros((2, body_own), F32)], 0
    )
    motion_all[me] = motion_own[...]

    for x in range(span_x):
        if x % chunk == 0:
            pop_in[x // chunk].wait()
        for z in range(0, span_z, 8):
            f = [pop[d, x, z : z + 8, :] for d in range(19)]
            rho = f[0]
            for d in range(1, 19):
                rho = rho + f[d]
            inv = 1.0 / rho
            u = []
            for c in range(3):
                pos, neg = dirs_of(c, 1), dirs_of(c, -1)
                tot = f[pos[0]] - f[neg[0]]
                for p, q in zip(pos[1:], neg[1:]):
                    tot = tot + (f[p] - f[q])
                u.append(tot * inv)
            usq = 1.0 - 1.5 * (u[0] * u[0] + u[1] * u[1] + u[2] * u[2])
            rows = pl.ds(x * span_z + z, 8)
            keep = 1.0 - OMEGA
            relaxed[0, rows, :] = keep * f[0] + (OMEGA * WT[0]) * rho * usq
            for d in range(1, 19, 2):
                terms = [u[c] if VEL[d][c] > 0 else -u[c] for c in range(3) if VEL[d][c]]
                proj = terms[0] if len(terms) == 1 else terms[0] + terms[1]
                scale = (OMEGA * WT[d]) * rho
                even = scale * (usq + 4.5 * proj * proj)
                odd = scale * (3.0 * proj)
                relaxed[d, rows, :] = keep * f[d] + (even + odd)
                relaxed[d + 1, rows, :] = keep * f[d + 1] + (even - odd)

    for s in range(2):
        xe = (span_x - 1) if s == 0 else 0
        ze = (span_z - 1) if s == 0 else 0
        for j, d in enumerate(XD[s]):
            sendx[s, j] = relaxed[d, xe * span_z : (xe + 1) * span_z, :]
        for j, d in enumerate(ZD[s]):
            for x in range(span_x):
                r = x * span_z + ze
                sendz[s, j, x : x + 1, :] = relaxed[d, r : r + 1, :]
        sende[s] = jnp.zeros(sende.shape[1:], F32)
        for j, d in enumerate(XZD[s]):
            r = xe * span_z + ((span_z - 1) if VEL[d][2] > 0 else 0)
            sende[s, j : j + 1, :] = relaxed[d, r : r + 1, :]
    lane = lax.broadcasted_iota(jnp.int32, (cells, span_y), 1)
    pack = jnp.zeros((cells, span_y), F32)
    for s in range(2):
        ye = (span_y - 1) if s == 0 else 0
        for j, d in enumerate(YD[s]):
            pack = jnp.where(lane == 8 * s + j, relaxed[d, :, ye : ye + 1], pack)
    pack_t = pack.T
    for s in range(2):
        sendy[s] = pack_t[8 * s : 8 * s + 8, :]

    pl.semaphore_wait(barrier, owners - 1 + len(others))

    def motion_copy(o, slot):
        return pltpu.make_async_remote_copy(
            src_ref=motion_own, dst_ref=motion_all.at[slot], send_sem=ms.at[o], recv_sem=mr.at[slot],
            device_id=peer_of(o)[1], device_id_type=pl.DeviceIdType.MESH,
        )

    loop(1, owners, lambda o: motion_copy(o, me).start())

    halo = []

    def rim(src, dst, target):
        k = len(halo)
        c = pltpu.make_async_remote_copy(
            src_ref=src, dst_ref=dst, send_sem=hs.at[k], recv_sem=hr.at[k],
            device_id=target, device_id_type=pl.DeviceIdType.MESH,
        )
        c.start()
        halo.append(c)

    for s in range(2):
        xt, yt = (ap, bp) if s == 0 else (am, bm)
        rim(sendx.at[s], xin.at[s], dev(xt, b, e))
        rim(sende.at[s], ein.at[s], dev(xt, b, oe))
        rim(sendy.at[s], yin.at[s, 0], dev(a, yt, e))
        rim(sendy.at[s], yin.at[s, 1], dev(ap, yt, e))
        rim(sendy.at[s], yin.at[s, 2], dev(am, yt, e))
        rim(sendy.at[s], yin.at[s, 3], dev(a, yt, oe))
    rim(sendz, zin, dev(a, b, oe))

    for k in (0, 1, 2, 3, 4, 5, 6, 9, 10):
        small_in[k].wait()

    cell = lcell[0, 0]
    dirs = ldir[0, 0]
    row_of = cell // span_y
    lane_of = cell - row_of * span_y
    dirs_f = dirs.astype(F32)
    iota_c = lax.broadcasted_iota(jnp.int32, (cells, links), 0)
    iota_y = lax.broadcasted_iota(jnp.int32, (span_y, links), 0)
    row_t = jnp.where(iota_c == row_of, 1.0, 0.0).astype(BF16)
    lane_mask = iota_y == lane_of
    dmap[...] = dot(row_t, jnp.where(lane_mask, dirs_f, 0.0).astype(BF16), 1, 1)
    dm = dmap[...]
    post_map = jnp.zeros((cells, span_y), F32)
    for d in range(1, 19):
        post_map = jnp.where(dm == float(d), relaxed[d], post_map)
    picked = None
    for part in split3(post_map):
        t = dot(part.astype(BF16), row_t, 0, 0)
        picked = t if picked is None else picked + t
    post = jnp.sum(jnp.where(lane_mask, picked, 0.0), axis=0, keepdims=True)
    iota_s = lax.broadcasted_iota(jnp.int32, (slots, links), 0)
    slot_t = jnp.where(iota_s == lslot[0, 0], 1.0, 0.0).astype(BF16)

    vel = []
    for c in range(3):
        v = jnp.zeros((1, links), F32)
        for d in range(1, 19):
            if VEL[d][c]:
                v = jnp.where(dirs == d, float(VEL[d][c]), v)
        vel.append(v)
    six_w = jnp.where(dirs > 6, 6.0 * WT[7], 6.0 * WT[1])

    def motion_wait(o):
        p, _ = peer_of(o)
        motion_copy(o, p).wait_recv()

    loop(1, owners, motion_wait)
    bodies = bb_ref[0, 0]
    iota_b = lax.broadcasted_iota(jnp.int32, (body_own, slots), 0)

    def owner_onehot(o):
        return jnp.where(iota_b == bodies - o * body_own, 1.0, 0.0).astype(BF16)

    def gather(o, acc):
        return acc + dot(stacked(motion_all[o]), owner_onehot(o), 1, 0)

    slot_motion = unstacked(
        lax.fori_loop(0, owners, gather, jnp.zeros((24, slots), F32), unroll=unroll)
    )
    m = unstacked(dot(stacked(slot_motion), slot_t, 1, 0))
    mv = [m[i : i + 1, :] for i in range(6)]
    arm = [larm[i, 0, 0] for i in range(3)]
    wall = [
        mv[0] + mv[4] * arm[2] - mv[5] * arm[1],
        mv[1] + mv[5] * arm[0] - mv[3] * arm[2],
        mv[2] + mv[3] * arm[1] - mv[4] * arm[0],
    ]
    drop = six_w * (vel[0] * wall[0] + vel[1] * wall[1] + vel[2] * wall[2])
    bounce = post - drop
    live = jnp.where(dirs > 0, 1.0, 0.0)
    exchanged = (post + bounce) * live
    force = [vel[c] * exchanged for c in range(3)]
    torque = [
        arm[1] * force[2] - arm[2] * force[1],
        arm[2] * force[0] - arm[0] * force[2],
        arm[0] * force[1] - arm[1] * force[0],
    ]
    loads = jnp.concatenate(force + torque + [jnp.zeros((2, links), F32)], 0)
    slot_load = unstacked(dot(stacked(loads), slot_t, 1, 1))
    slot_parts = stacked(slot_load)

    def spread(o):
        tiles[o] = unstacked(dot(slot_parts, owner_onehot(o), 1, 1))

    loop(0, owners, spread)

    def force_copy(o, src, slot):
        return pltpu.make_async_remote_copy(
            src_ref=tiles.at[src], dst_ref=force_all.at[slot], send_sem=fs.at[o], recv_sem=fr.at[slot],
            device_id=peer_of(o)[1], device_id_type=pl.DeviceIdType.MESH,
        )

    loop(1, owners, lambda o: force_copy(o, peer_of(o)[0], me).start())
    force_all[me] = tiles[me]

    wm = None
    for part in split3(drop):
        t = dot(row_t, jnp.where(lane_mask, part, 0.0).astype(BF16), 1, 1)
        wm = t if wm is None else wm + t
    wmap[...] = wm

    for c in halo:
        c.wait_recv()
    lane_c = lax.broadcasted_iota(jnp.int32, (8, cells), 1)
    z_c = lane_c - (lane_c // span_z) * span_z
    sub_c = lax.broadcasted_iota(jnp.int32, (8, cells), 0)
    both = []
    for s in range(2):
        t0, t1, t2, t3 = (yin[s, k] for k in range(4))
        out = t0
        for j, d in enumerate(YD[s]):
            cx, _, cz = VEL[d]
            if cx == 1:
                v = jnp.where(lane_c < span_z, pltpu.roll(t1, span_z, 1), pltpu.roll(t0, span_z, 1))
            elif cx == -1:
                v = jnp.where(
                    lane_c >= cells - span_z,
                    pltpu.roll(t2, cells - span_z, 1),
                    pltpu.roll(t0, cells - span_z, 1),
                )
            elif cz == 1:
                v = jnp.where(z_c == 0, pltpu.roll(t3, cells - span_z + 1, 1), pltpu.roll(t0, 1, 1))
            elif cz == -1:
                v = jnp.where(
                    z_c == span_z - 1, pltpu.roll(t3, span_z - 1, 1), pltpu.roll(t0, cells - 1, 1)
                )
            else:
                continue
            out = jnp.where(sub_c == j, v, out)
        both.append(out)
    both.append(jnp.zeros((span_y - 16, cells), F32))
    ycols[...] = jnp.concatenate(both, 0).T

    iz = lax.broadcasted_iota(jnp.int32, (span_z, span_y), 0)
    iy = lax.broadcasted_iota(jnp.int32, (span_z, span_y), 1)
    for x in range(span_x):
        rows = slice(x * span_z, (x + 1) * span_z)
        dm_x = dmap[rows, :]
        wm_x = wmap[rows, :]
        for i in range(19):
            cx, cy, cz = VEL[i]
            sx = x - cx
            inside = 0 <= sx < span_x
            if inside:
                v = relaxed[i, sx * span_z : (sx + 1) * span_z, :]
            else:
                s = 0 if cx > 0 else 1
                v = xin[s, XD[s].index(i)]
            if cz:
                s = 0 if cz > 0 else 1
                if inside:
                    edge = zin[s, ZD[s].index(i), sx : sx + 1, :]
                else:
                    sxx = 0 if cx > 0 else 1
                    j = XZD[sxx].index(i)
                    edge = ein[sxx, j : j + 1, :]
                v = pltpu.roll(v, 1 if cz > 0 else span_z - 1, 0)
                v = jnp.where(iz == (0 if cz > 0 else span_z - 1), edge, v)
            if cy:
                s = 0 if cy > 0 else 1
                j = 8 * s + YD[s].index(i)
                v = pltpu.roll(v, 1 if cy > 0 else span_y - 1, 1)
                v = jnp.where(iy == (0 if cy > 0 else span_y - 1), ycols[rows, j : j + 1], v)
            if i:
                d = OPP[i]
                v = jnp.where(dm_x == float(d), relaxed[d, rows, :] - wm_x, v)
            nxt[i, x] = v

    def force_wait(o):
        p, _ = peer_of(o)
        force_copy(o, p, p).wait_recv()

    loop(1, owners, force_wait)
    half[...] = lax.fori_loop(
        0, owners, lambda o, acc: acc + force_all[o], jnp.zeros(half.shape, F32), unroll=unroll
    )
    swap = pltpu.make_async_remote_copy(
        src_ref=half, dst_ref=half_in, send_sem=cs, recv_sem=cr,
        device_id=dev(a, b, oe), device_id_type=pl.DeviceIdType.MESH,
    )
    swap.start()

    def sent(o):
        motion_copy(o, me).wait_send()
        force_copy(o, peer_of(o)[0], me).wait_send()

    loop(1, owners, sent)
    for c in halo:
        c.wait_send()
    swap.wait()
    load = half[...] + half_in[...]
    f = [load[i : i + 1, :] for i in range(6)]
    pos = [bpos[i : i + 1, :] for i in range(3)]
    qw, qx, qy, qz = (bquat[i : i + 1, :] for i in range(4))
    velo = [bvel[i : i + 1, :] + imass[...] * f[i] for i in range(3)]
    velo[2] = velo[2] - GRAV
    rot = [
        [1.0 - 2.0 * (qy * qy + qz * qz), 2.0 * (qx * qy - qw * qz), 2.0 * (qx * qz + qw * qy)],
        [2.0 * (qx * qy + qw * qz), 1.0 - 2.0 * (qx * qx + qz * qz), 2.0 * (qy * qz - qw * qx)],
        [2.0 * (qx * qz - qw * qy), 2.0 * (qy * qz + qw * qx), 1.0 - 2.0 * (qx * qx + qy * qy)],
    ]
    tq = f[3:6]
    acc = [
        iinert[c : c + 1, :] * (rot[0][c] * tq[0] + rot[1][c] * tq[1] + rot[2][c] * tq[2])
        for c in range(3)
    ]
    spin = [
        bspin[r : r + 1, :] + (rot[r][0] * acc[0] + rot[r][1] * acc[1] + rot[r][2] * acc[2])
        for r in range(3)
    ]
    sx, sy, sz = spin
    dq = [
        -(sx * qx + sy * qy + sz * qz),
        sx * qw + sy * qz - sz * qy,
        sy * qw + sz * qx - sx * qz,
        sz * qw + sx * qy - sy * qx,
    ]
    scale = lax.rsqrt(1.0 + 0.25 * (sx * sx + sy * sy + sz * sz))
    quat = [(q + 0.5 * k) * scale for q, k in zip((qw, qx, qy, qz), dq)]
    result = [pos[i] + velo[i] for i in range(3)] + quat + velo + spin
    for i, v in enumerate(result):
        bnext[i : i + 1, :] = v


def write_out(a, b, a_out, b_out, sems):
    copies = [pltpu.make_async_copy(a, a_out, sems.at[0]), pltpu.make_async_copy(b, b_out, sems.at[1])]
    for c in copies:
        c.start()
    for c in copies:
        c.wait()


def shards(sizes, *args):
    pop = args[0]
    span_x, span_z, span_y = pop.shape[1:]
    cells = span_x * span_z
    body_own = args[6].shape[1]
    owners = sizes[0] * sizes[1]
    args = list(args)
    args[10] = args[10].reshape(1, -1)
    vm = pl.BlockSpec(memory_space=pltpu.VMEM)
    dma = pltpu.SemaphoreType.DMA
    V = lambda *s: pltpu.VMEM(s, F32)
    args = [pltpu.with_memory_space_constraint(v, pltpu.MemorySpace.HBM) for v in args]
    hbm = pl.BlockSpec(memory_space=pltpu.MemorySpace.HBM)
    outs = pl.pallas_call(
        functools.partial(kernel, sizes),
        out_shape=(
            jax.ShapeDtypeStruct(pop.shape, F32),
            jax.ShapeDtypeStruct((13, body_own), F32),
        ),
        in_specs=[hbm] * len(args),
        out_specs=(vm, vm),
        scratch_shapes=[
            *[pltpu.VMEM(v.shape, v.dtype) for v in args],
            V(19, cells, span_y),
            V(2, 5, span_z, span_y), V(2, 5, span_z, span_y),
            V(2, 5, span_x, span_y), V(2, 5, span_x, span_y),
            V(2, 8, span_y), V(2, 8, span_y),
            V(2, 8, cells), V(2, 4, 8, cells),
            V(16, cells), V(cells, span_y),
            V(cells, span_y), V(cells, span_y),
            V(8, body_own), V(owners, 8, body_own),
            V(owners, 8, body_own), V(owners, 8, body_own),
            V(8, body_own), V(8, body_own),
            dma((13,)), dma((13,)),
            dma((owners,)), dma((owners,)),
            dma((owners,)), dma((owners,)),
            dma, dma,
            dma((POP_CHUNKS,)), dma((11,)),
        ],
        compiler_params=pltpu.CompilerParams(
            collective_id=0, has_side_effects=True, vmem_limit_bytes=K1_VMEM
        ),
        name="lattice_step",
    )(*args)
    return pl.pallas_call(
        write_out,
        out_shape=tuple(jax.ShapeDtypeStruct(v.shape, F32) for v in outs),
        in_specs=[vm, vm],
        out_specs=(hbm, hbm),
        scratch_shapes=[dma((2,))],
        compiler_params=pltpu.CompilerParams(vmem_limit_bytes=K2_VMEM),
        name="write_out",
    )(*outs)


def solution(mesh):
    sizes = (mesh.shape["gx"], mesh.shape["gy"])
    link = P("gx", "gz", "gy", None)
    body = P(None, ("gx", "gy"))
    return jax.shard_map(
        functools.partial(shards, sizes),
        mesh=mesh,
        in_specs=(
            P(None, "gx", "gz", "gy"), link, link, link, P(None, "gx", "gz", "gy", None), link,
            body, body, body, body, P(("gx", "gy")), body,
        ),
        out_specs=(P(None, "gx", "gz", "gy"), body),
        check_vma=False,
    )
```

profile of v0, /device:TPU:0, one launch (start us, length us, event | category | flops | bytes accessed | tf_op | source)
XLA Modules:
  0.0 21.2 jit_solution(15577707202083543986)
XLA Ops:
  0.6 19.5 %lattice_step.1 = (f32[19,8,16,128]{3,2,1,0:T(8,128)S(1)}, f32[13,128]{1,0:T(8,128)S(1)}) custom-call(f32[19,8,16,128]{3,2,1,0:T(8,128)} %pop_h.1, s32[1,1,1,1024]{3,2,1,0:T(1,128)} %rest_0_.1, s32[1,1,1,1024]{3,2,1,0:T(1,128)} %rest_1_.1, s32[1,1,1,1024]{3,2,1,0:T(1,128)} %rest_2_.1, f32[3,1,1,1,1024]{4,3,2,1,0:T(1,128)} %rest_3_.1, ...), custom_call_target="tpu_custom_call" | custom-call | tf_op jit(solution)/shard_map/lattice_step/pallas_call | solution.py:458
  20.1 1.1 %write_out.1 = (f32[19,8,16,128]{3,2,1,0:T(8,128)}, f32[13,128]{1,0:T(8,128)}) custom-call(f32[19,8,16,128]{3,2,1,0:T(8,128)S(1)} %get-tuple-element.4.a, f32[13,128]{1,0:T(8,128)S(1)} %get-tuple-element.5.b), custom_call_target="tpu_custom_call" | custom-call | tf_op jit(solution)/shard_map/write_out/pallas_call | solution.py:489
where the time goes:
time: 21.4 us; the launch traced here: 21.2 us
  Pallas kernels  20.5 us (96%)
  between operations  0.64 us (3%)
    pallas_call x1, Pallas kernels, shards(): pl.pallas_call(functools.partial(kernel, sizes), out_shape=(jax.ShapeDtyp...  19.5 us
    pallas_call x1, Pallas kernels, shards(): pl.pallas_call(write_out, out_shape=tuple((jax.ShapeDtypeStruct(v.shape,...  1.06 us

commit v1 on v0

--- a/solution.py
+++ b/solution.py
@@ -263,12 +263,14 @@
     def owner_onehot(o):
         return jnp.where(iota_b == bodies - o * body_own, 1.0, 0.0).astype(BF16)
 
+    owner_of = bodies // body_own
+    local_of = jnp.broadcast_to(bodies - owner_of * body_own, (8, slots))
+
     def gather(o, acc):
-        return acc + dot(stacked(motion_all[o]), owner_onehot(o), 1, 0)
-
-    slot_motion = unstacked(
-        lax.fori_loop(0, owners, gather, jnp.zeros((24, slots), F32), unroll=unroll)
-    )
+        g = jnp.take_along_axis(motion_all[o], local_of, axis=1)
+        return jnp.where(owner_of == o, g, acc)
+
+    slot_motion = lax.fori_loop(0, owners, gather, jnp.zeros((8, slots), F32), unroll=unroll)
     m = unstacked(dot(stacked(slot_motion), slot_t, 1, 0))
     mv = [m[i : i + 1, :] for i in range(6)]
     arm = [larm[i, 0, 0] for i in range(3)]

time: 21.4 us -> 21.1 us (0.986)
    pallas_call x1, Pallas kernels: 19.5 us -> 19.2 us  [shards(): pl.pallas_call(functools.partial(kernel, sizes), out_shape=(jax.ShapeDtyp...]
where the time goes in v1:
time: 21.1 us; the launch traced here: 20.9 us
  Pallas kernels  20.3 us (96%)
  between operations  0.64 us (3%)
    pallas_call x1, Pallas kernels, shards(): pl.pallas_call(functools.partial(kernel, sizes), out_shape=(jax.ShapeDtyp...  19.2 us
    pallas_call x1, Pallas kernels, shards(): pl.pallas_call(write_out, out_shape=tuple((jax.ShapeDtypeStruct(v.shape,...  1.06 us

profile of v1, /device:TPU:0, one launch (start us, length us, event | category | flops | bytes accessed | tf_op | source)
XLA Modules:
  0.0 20.9 jit_solution(3328571770550131220)
XLA Ops:
  0.6 19.2 %lattice_step.1 = (f32[19,8,16,128]{3,2,1,0:T(8,128)S(1)}, f32[13,128]{1,0:T(8,128)S(1)}) custom-call(f32[19,8,16,128]{3,2,1,0:T(8,128)} %pop_h.1, s32[1,1,1,1024]{3,2,1,0:T(1,128)} %rest_0_.1, s32[1,1,1,1024]{3,2,1,0:T(1,128)} %rest_1_.1, s32[1,1,1,1024]{3,2,1,0:T(1,128)} %rest_2_.1, f32[3,1,1,1,1024]{4,3,2,1,0:T(1,128)} %rest_3_.1, ...), custom_call_target="tpu_custom_call" | custom-call | tf_op jit(solution)/shard_map/lattice_step/pallas_call | solution.py:460
  19.9 1.1 %write_out.1 = (f32[19,8,16,128]{3,2,1,0:T(8,128)}, f32[13,128]{1,0:T(8,128)}) custom-call(f32[19,8,16,128]{3,2,1,0:T(8,128)S(1)} %get-tuple-element.4.a, f32[13,128]{1,0:T(8,128)S(1)} %get-tuple-element.5.b), custom_call_target="tpu_custom_call" | custom-call | tf_op jit(solution)/shard_map/write_out/pallas_call | solution.py:491

commit v2 on v0

v2 whole, which is shorter than its diff:
```python
import functools

import jax
import jax.numpy as jnp
import numpy as np
from jax import lax
from jax.experimental import pallas as pl
from jax.experimental.pallas import tpu as pltpu
from jax.sharding import PartitionSpec as P

VEL = [
    (0, 0, 0), (1, 0, 0), (-1, 0, 0), (0, 1, 0), (0, -1, 0), (0, 0, 1), (0, 0, -1),
    (1, 1, 0), (-1, -1, 0), (1, -1, 0), (-1, 1, 0), (1, 0, 1), (-1, 0, -1), (1, 0, -1),
    (-1, 0, 1), (0, 1, 1), (0, -1, -1), (0, 1, -1), (0, -1, 1),
]
WT = [1.0 / 3.0] + [1.0 / 18.0] * 6 + [1.0 / 36.0] * 12
OPP = [0, 2, 1, 4, 3, 6, 5, 8, 7, 10, 9, 12, 11, 14, 13, 16, 15, 18, 17]
OMEGA = 1.25
POP_CHUNKS = 4
K1_VMEM = 24 * 1024 * 1024
K2_VMEM = 4 * 1024 * 1024
GRAV = 0.02
F32 = jnp.float32
BF16 = jnp.bfloat16
I32 = jnp.int32
SUB = 8
PAIRS = [(i, j) for i in range(6) for j in range(i, 6)]
NA = 6
NM = len(PAIRS)
NM_PAD = 24


def dirs_of(comp, sign):
    return [d for d in range(19) if VEL[d][comp] == sign]


XD = (dirs_of(0, 1), dirs_of(0, -1))
YD = (dirs_of(1, 1), dirs_of(1, -1))
ZD = (dirs_of(2, 1), dirs_of(2, -1))
XZD = tuple([d for d in XD[s] if VEL[d][2] != 0] for s in range(2))


def dot(a, b, ca, cb):
    return lax.dot_general(a, b, (((ca,), (cb,)), ((), ())), preferred_element_type=F32)


def stacked(v):
    hi = v.astype(BF16).astype(F32)
    return jnp.concatenate([hi, v - hi], 0).astype(BF16)


def unstacked(v):
    k = v.shape[0] // 2
    return v[0:k] + v[k : 2 * k]


def pick(table, index):
    index = jnp.clip(index, 0, table.shape[1] - 1)
    return jnp.take_along_axis(table, index, axis=1, mode="promise_in_bounds")


def spread(row, like):
    return jnp.broadcast_to(row, like.shape)


def kernel(
    sizes,
    pop_h, *rest,
):
    small_h, outs, rest = rest[:11], rest[11:15], rest[15:]
    pop, small, rest = rest[0], rest[1:12], rest[12:]
    step(sizes, pop_h, small_h, pop, *small, *outs, *rest)


def step(
    sizes, pop_h, small_h,
    pop, lcell, ldir, lslot, larm, bb_ref, bpos, bquat, bvel, bspin, imass, iinert,
    nxt, state, got_m, got_a,
    relaxed, sendx, xin, sendz, zin, sende, ein, sendy, yin, ycols,
    post_map, dmap, links_f, comps_m, comps_a, place_hot, row_hot, slot_m, slot_a,
    motion_own, motion_all, send_m, recv_m, send_a, recv_a,
    hs, xr, er, yr, zr, ms, mr, rs, rr, fs, fr, ps, ss,
):
    ngx, ngy, cap = sizes
    owners = ngx * ngy
    devices = 2 * owners
    span_x, span_z, span_y = pop.shape[1:]
    cells = span_x * span_z
    body_own = bvel.shape[1]
    slots = bb_ref.shape[-1]
    chunks = lcell.shape[0]
    per_row = slots // cap
    m_rows = recv_m.shape[1] - 1
    a, b, e = lax.axis_index("gx"), lax.axis_index("gy"), lax.axis_index("gz")
    me = a * ngy + b
    own = me * 2 + e
    ap, am = lax.rem(a + 1, ngx), lax.rem(a + ngx - 1, ngx)
    bp, bm = lax.rem(b + 1, ngy), lax.rem(b + ngy - 1, ngy)
    oe = 1 - e

    def dev(x, y, z):
        return {"gx": x, "gy": y, "gz": z}

    def peer_of(offset, z):
        p = lax.rem(me + offset, owners)
        return p, dev(p // ngy, lax.rem(p, ngy), z)

    unroll = owners <= 16

    def loop(lo, hi, body):
        if unroll:
            for i in range(lo, hi):
                body(i)
        else:
            pl.loop(lo, hi)(body)

    def remote(src, dst, send_sem, recv_sem, target):
        return pltpu.make_async_remote_copy(
            src_ref=src, dst_ref=dst, send_sem=send_sem, recv_sem=recv_sem,
            device_id=target, device_id_type=pl.DeviceIdType.MESH,
        )

    def wait_bytes(ref, sem):
        pltpu.make_async_copy(ref, ref, sem).wait()

    small = (lcell, ldir, lslot, larm, bb_ref, bpos, bquat, bvel, bspin, imass, iinert)
    small_in = [
        pltpu.make_async_copy(src, dst, ss.at[k]) for k, (src, dst) in enumerate(zip(small_h, small))
    ]
    chunk = span_x // POP_CHUNKS
    pop_in = [
        pltpu.make_async_copy(
            pop_h.at[:, pl.ds(k * chunk, chunk)], pop.at[:, pl.ds(k * chunk, chunk)], ps.at[k]
        )
        for k in range(POP_CHUNKS)
    ]
    for k in (4, 0, 1, 2, 3):
        small_in[k].start()
    for c in pop_in:
        c.start()
    for k in (7, 8, 5, 6, 9, 10):
        small_in[k].start()

    barrier = pltpu.get_barrier_semaphore()

    def greet(o):
        for z in (e, oe):
            pl.semaphore_signal(
                barrier, inc=1, device_id=peer_of(o, z)[1], device_id_type=pl.DeviceIdType.MESH
            )

    loop(1, owners, greet)
    pl.semaphore_signal(
        barrier, inc=1, device_id=dev(a, b, oe), device_id_type=pl.DeviceIdType.MESH
    )

    tile = (SUB, span_y)
    lane_t = lax.broadcasted_iota(I32, tile, 1)
    sub_t = lax.broadcasted_iota(I32, tile, 0)

    small_in[4].wait()
    bodies = bb_ref[...]
    owner_row = bodies // body_own
    local_row = bodies - owner_row * body_own
    sq = (slots, slots)
    owner_b = jnp.broadcast_to(owner_row.astype(F32), sq)
    iota_0 = lax.broadcasted_iota(I32, sq, 0)
    iota_1 = lax.broadcasted_iota(I32, sq, 1)
    earlier = jnp.where((owner_b == owner_b.T) & (iota_0 < iota_1), 1.0, 0.0)
    rank_row = jnp.sum(earlier, axis=0, keepdims=True)
    iota_o = lax.broadcasted_iota(I32, (owners, slots), 0)
    owned = iota_o == owner_row
    by_owner = jnp.where(owned, rank_row + 1.0, 0.0).astype(BF16)
    place = jnp.where(iota_0 == local_row, 1.0, 0.0).astype(BF16)
    rank_of = dot(by_owner, place, 1, 1)
    place_row = owner_row * cap + rank_row.astype(I32)
    for o in range(owners):
        send_m[o, m_rows : m_rows + 1, :] = rank_of[o : o + 1, :]
    lane_block = lane_t // cap
    unpack = sub_t * cap + lane_t - lane_block * cap

    def pack(src, count, dst):
        for g in range(owners // SUB):
            first = g * SUB * cap
            half = slice(first // slots * slots, first // slots * slots + slots)
            index = unpack + first % slots
            for r in range(-(-count // per_row)):
                out = jnp.zeros(tile, F32)
                for k in range(min(per_row, count - r * per_row)):
                    c = r * per_row + k
                    got = pick(spread(src[c : c + 1, half], out), index)
                    out = jnp.where(lane_block == k, got, out)
                for s in range(SUB):
                    dst[g * SUB + s, r : r + 1, :] = out[s : s + 1, :]

    for k in (0, 1, 2, 3):
        small_in[k].wait()
    cell = lcell[...]
    dirs = ldir[...]
    slot = lslot[...]
    row_of = cell // span_y
    lane_of = cell - row_of * span_y
    vel = []
    for c in range(3):
        v = jnp.zeros(tile, F32)
        for d in range(1, 19):
            if VEL[d][c]:
                v = jnp.where(dirs == d, float(VEL[d][c]), v)
        vel.append(v)
    six_w = jnp.where(dirs > 6, 6.0 * WT[7], 6.0 * WT[1])
    arm = [larm[SUB * i : SUB * (i + 1), :] for i in range(3)]
    f6 = vel + [
        arm[1] * vel[2] - arm[2] * vel[1],
        arm[2] * vel[0] - arm[0] * vel[2],
        arm[0] * vel[1] - arm[1] * vel[0],
    ]
    for q in range(6):
        links_f[q] = f6[q]
    links_f[6] = six_w
    wf = [six_w * v for v in f6]

    def by_chunk(comps, q, value):
        for j in range(chunks):
            comps[j, q : q + 1, :] = value[j : j + 1, :]

    for q, (i, j) in enumerate(PAIRS):
        by_chunk(comps_m, q, wf[i] * f6[j])
    for j in range(chunks):
        comps_m[j, NM:NM_PAD, :] = jnp.zeros((NM_PAD - NM, span_y), F32)
        comps_a[j, NA:SUB, :] = jnp.zeros((SUB - NA, span_y), F32)
    link_place = pick(spread(place_row, slot), slot)
    iota_p = lax.broadcasted_iota(I32, (owners * cap, span_y), 0)
    for j in range(chunks):
        place_hot[:, j * span_y : (j + 1) * span_y] = jnp.where(
            iota_p == link_place[j : j + 1, :], 1.0, 0.0
        ).astype(BF16)

    def slot_sums(comps):
        v = jnp.concatenate([comps[j] for j in range(chunks)], 1)
        return unstacked(dot(stacked(v), place_hot[...], 1, 1))

    slot_m[...] = slot_sums(comps_m)
    pack(slot_m, NM, send_m)

    iota_c = lax.broadcasted_iota(I32, (cells, span_y), 0)
    iota_y = lax.broadcasted_iota(I32, (span_y, span_y), 0)

    def at_lanes(value):
        return jnp.concatenate(
            [
                jnp.where(iota_y == lane_of[j : j + 1, :], value[j : j + 1, :], 0.0).astype(BF16)
                for j in range(chunks)
            ],
            1,
        )

    for j in range(chunks):
        row_hot[:, j * span_y : (j + 1) * span_y] = jnp.where(
            iota_c == row_of[j : j + 1, :], 1.0, 0.0
        ).astype(BF16)
    dmap[...] = dot(row_hot[...], at_lanes(dirs.astype(F32)), 1, 1).astype(I32)

    for x in range(span_x):
        if x % chunk == 0:
            pop_in[x // chunk].wait()
        for z in range(0, span_z, SUB):
            f = [pop[d, x, z : z + SUB, :] for d in range(19)]
            rho = f[0]
            for d in range(1, 19):
                rho = rho + f[d]
            inv = 1.0 / rho
            u = []
            for c in range(3):
                pos, neg = dirs_of(c, 1), dirs_of(c, -1)
                tot = f[pos[0]] - f[neg[0]]
                for p, q in zip(pos[1:], neg[1:]):
                    tot = tot + (f[p] - f[q])
                u.append(tot * inv)
            usq = 1.0 - 1.5 * (u[0] * u[0] + u[1] * u[1] + u[2] * u[2])
            rows = pl.ds(x * span_z + z, SUB)
            keep = 1.0 - OMEGA
            relaxed[0, rows, :] = keep * f[0] + (OMEGA * WT[0]) * rho * usq
            at = dmap[rows, :]
            post = jnp.zeros(tile, F32)
            for d in range(1, 19, 2):
                terms = [u[c] if VEL[d][c] > 0 else -u[c] for c in range(3) if VEL[d][c]]
                proj = terms[0] if len(terms) == 1 else terms[0] + terms[1]
                scale = (OMEGA * WT[d]) * rho
                even = scale * (usq + 4.5 * proj * proj)
                odd = scale * (3.0 * proj)
                v = keep * f[d] + (even + odd)
                relaxed[d, rows, :] = v
                post = jnp.where(at == d, v, post)
                v = keep * f[d + 1] + (even - odd)
                relaxed[d + 1, rows, :] = v
                post = jnp.where(at == d + 1, v, post)
            post_map[rows, :] = post

    lane = lax.broadcasted_iota(I32, (cells, span_y), 1)
    packed = jnp.zeros((cells, span_y), F32)
    for s in range(2):
        ye = (span_y - 1) if s == 0 else 0
        for j, d in enumerate(YD[s]):
            packed = jnp.where(lane == 8 * s + j, relaxed[d, :, ye : ye + 1], packed)
    pack_t = packed.T
    for s in range(2):
        sendy[s] = pack_t[8 * s : 8 * s + 8, :]
    for s in range(2):
        xe = (span_x - 1) if s == 0 else 0
        ze = (span_z - 1) if s == 0 else 0
        for j, d in enumerate(XD[s]):
            sendx[s, j] = relaxed[d, xe * span_z : (xe + 1) * span_z, :]
        for j, d in enumerate(ZD[s]):
            for x in range(span_x):
                r = x * span_z + ze
                sendz[s, j, x : x + 1, :] = relaxed[d, r : r + 1, :]
        sende[s] = jnp.zeros(sende.shape[1:], F32)
        for j, d in enumerate(XZD[s]):
            r = xe * span_z + ((span_z - 1) if VEL[d][2] > 0 else 0)
            sende[s, j : j + 1, :] = relaxed[d, r : r + 1, :]

    small_in[7].wait()
    small_in[8].wait()
    motion_own[...] = jnp.concatenate(
        [bvel[...], bspin[...], jnp.zeros((2, body_own), F32)], 0
    )
    motion_all[me] = motion_own[...]
    recv_m[own] = send_m[me]

    pl.semaphore_wait(barrier, devices - 1)

    for s in range(2):
        xt, yt = (ap, bp) if s == 0 else (am, bm)
        for k, t in enumerate((dev(a, yt, e), dev(ap, yt, e), dev(am, yt, e), dev(a, yt, oe))):
            remote(sendy.at[s], yin.at[s, k], hs, yr, t).start()
        remote(sendx.at[s], xin.at[s], hs, xr, dev(xt, b, e)).start()
        remote(sende.at[s], ein.at[s], hs, er, dev(xt, b, oe)).start()
    remote(sendz, zin, hs, zr, dev(a, b, oe)).start()

    def send_motion(o):
        remote(motion_own, motion_all.at[me], ms, mr, peer_of(o, e)[1]).start()

    loop(1, owners, send_motion)

    def send_response(o):
        for z in (e, oe):
            p, target = peer_of(o, z)
            remote(send_m.at[p], recv_m.at[own], rs, rr, target).start()

    loop(1, owners, send_response)
    remote(send_m.at[me], recv_m.at[own], rs, rr, dev(a, b, oe)).start()

    parts = [jnp.zeros(tile, F32) for _ in range(4)]
    for r in range(cells):
        got = pick(spread(post_map[r : r + 1, :], parts[0]), lane_of)
        parts[r % 4] = jnp.where(row_of == r, got, parts[r % 4])
    post2 = 2.0 * ((parts[0] + parts[1]) + (parts[2] + parts[3]))
    for q in range(NA):
        by_chunk(comps_a, q, post2 * links_f[q])
    slot_a[...] = slot_sums(comps_a)
    pack(slot_a, NA, send_a)
    recv_a[own] = send_a[me]

    def send_push(o):
        for z in (e, oe):
            p, target = peer_of(o, z)
            remote(send_a.at[p], recv_a.at[own], fs, fr, target).start()

    loop(1, owners, send_push)
    remote(send_a.at[me], recv_a.at[own], fs, fr, dev(a, b, oe)).start()

    for k in (5, 6, 9, 10):
        small_in[k].wait()
    wait_bytes(xin, xr)
    wait_bytes(ein, er)
    wait_bytes(zin, zr)
    iz = lax.broadcasted_iota(I32, (span_z, span_y), 0)
    iy = lax.broadcasted_iota(I32, (span_z, span_y), 1)
    for x in range(span_x):
        for i in range(19):
            cx, cy, cz = VEL[i]
            sx = x - cx
            inside = 0 <= sx < span_x
            if inside:
                v = relaxed[i, sx * span_z : (sx + 1) * span_z, :]
            else:
                s = 0 if cx > 0 else 1
                v = xin[s, XD[s].index(i)]
            if cz:
                s = 0 if cz > 0 else 1
                if inside:
                    edge = zin[s, ZD[s].index(i), sx : sx + 1, :]
                else:
                    sxx = 0 if cx > 0 else 1
                    j = XZD[sxx].index(i)
                    edge = ein[sxx, j : j + 1, :]
                v = pltpu.roll(v, 1 if cz > 0 else span_z - 1, 0)
                v = jnp.where(iz == (0 if cz > 0 else span_z - 1), edge, v)
            if cy:
                v = pltpu.roll(v, 1 if cy > 0 else span_y - 1, 1)
            nxt[i, x] = v

    state[0:16, :] = jnp.concatenate(
        [bpos[...], bquat[...], bvel[...], bspin[...], iinert[...]], 0
    )
    state[16:17, :] = imass[...]

    wait_bytes(motion_all.at[pl.ds(0, owners - 1)], mr)
    local_b = spread(local_row, lane_t)

    def gather_motion(o, acc):
        return jnp.where(owner_row == o, pick(motion_all[o], local_b), acc)

    slot_motion = lax.fori_loop(0, owners, gather_motion, jnp.zeros(tile, F32), unroll=unroll)
    along = None
    for q in range(6):
        t = links_f[q] * pick(spread(slot_motion[q : q + 1, :], slot), slot)
        along = t if along is None else along + t
    drop = links_f[6] * along
    drop_hi = drop.astype(BF16).astype(F32)
    drops = jnp.concatenate([at_lanes(drop_hi), at_lanes(drop - drop_hi)], 0)
    wall = dot(row_hot[...], drops, 1, 1)
    post_map[...] = post_map[...] - (wall[:, 0:span_y] + wall[:, span_y : 2 * span_y])

    wait_bytes(yin, yr)
    lane_c = lax.broadcasted_iota(I32, (8, cells), 1)
    z_c = lane_c - (lane_c // span_z) * span_z
    sub_c = lax.broadcasted_iota(I32, (8, cells), 0)
    both = []
    for s in range(2):
        t0, t1, t2, t3 = (yin[s, k] for k in range(4))
        out = t0
        for j, d in enumerate(YD[s]):
            cx, _, cz = VEL[d]
            if cx == 1:
                v = jnp.where(lane_c < span_z, pltpu.roll(t1, span_z, 1), pltpu.roll(t0, span_z, 1))
            elif cx == -1:
                v = jnp.where(
                    lane_c >= cells - span_z,
                    pltpu.roll(t2, cells - span_z, 1),
                    pltpu.roll(t0, cells - span_z, 1),
                )
            elif cz == 1:
                v = jnp.where(z_c == 0, pltpu.roll(t3, cells - span_z + 1, 1), pltpu.roll(t0, 1, 1))
            elif cz == -1:
                v = jnp.where(
                    z_c == span_z - 1, pltpu.roll(t3, span_z - 1, 1), pltpu.roll(t0, cells - 1, 1)
                )
            else:
                continue
            out = jnp.where(sub_c == j, v, out)
        both.append(out)
    both.append(jnp.zeros((span_y - 16, cells), F32))
    ycols[...] = jnp.concatenate(both, 0).T

    for x in range(span_x):
        rows = slice(x * span_z, (x + 1) * span_z)
        at = dmap[rows, :]
        bounce = post_map[rows, :]
        for i in range(1, 19):
            cy = VEL[i][1]
            v = nxt[i, x]
            if cy:
                s = 0 if cy > 0 else 1
                j = 8 * s + YD[s].index(i)
                v = jnp.where(iy == (0 if cy > 0 else span_y - 1), ycols[rows, j : j + 1], v)
            nxt[i, x] = jnp.where(at == OPP[i], bounce, v)

    wait_bytes(sendx, hs)
    wait_bytes(sende, hs)
    wait_bytes(yin, hs)
    wait_bytes(sendz, hs)
    wait_bytes(motion_all.at[pl.ds(0, owners - 1)], ms)
    wait_bytes(recv_m.at[pl.ds(0, devices - 1)], rs)
    wait_bytes(recv_a.at[pl.ds(0, devices - 1)], fs)

    wait_bytes(recv_m.at[pl.ds(0, devices - 1)], rr)
    wait_bytes(recv_a.at[pl.ds(0, devices - 1)], fr)
    got_m[...] = recv_m[...]
    got_a[...] = recv_a[...]


def finish(cap, nxt, state, got_m, got_a, a_out, b_out, result, sems):
    out = pltpu.make_async_copy(nxt, a_out, sems.at[0])
    out.start()
    devices, slots = got_a.shape[0], got_a.shape[2]
    per_row = slots // cap
    m_rows = got_m.shape[1] - 1
    groups = NM_PAD // SUB
    sub_t = lax.broadcasted_iota(I32, (SUB, slots), 0)

    def gather(k, acc):
        rank = spread(got_m[k, m_rows : m_rows + 1, :], sub_t).astype(I32) - 1
        known = rank >= 0
        safe = sub_t * cap + jnp.clip(rank, 0, cap - 1)
        added = []
        for g in range(groups):
            r, base = (g * SUB) // per_row, (g * SUB) % per_row
            added.append(pick(spread(got_m[k, r : r + 1, :], safe), safe + base * cap))
        added.append(pick(spread(got_a[k], safe), safe))
        return tuple(v + jnp.where(known, w, 0.0) for v, w in zip(acc, added))

    zero = jnp.zeros((SUB, slots), F32)
    sums = lax.fori_loop(0, devices, gather, (zero,) * (groups + 1), unroll=devices <= 32)
    f = [sums[groups][i : i + 1, :] for i in range(6)]
    u = [state[7 + i : 8 + i, :] for i in range(6)]
    for q, (i, j) in enumerate(PAIRS):
        m = sums[q // SUB][q % SUB : q % SUB + 1, :]
        f[i] = f[i] - m * u[j]
        if i != j:
            f[j] = f[j] - m * u[i]
    pos = [state[i : i + 1, :] for i in range(3)]
    qw, qx, qy, qz = (state[3 + i : 4 + i, :] for i in range(4))
    vel, turn = u[0:3], u[3:6]
    inert = [state[13 + i : 14 + i, :] for i in range(3)]
    imass = state[16:17, :]
    velo = [vel[i] + imass * f[i] for i in range(3)]
    velo[2] = velo[2] - GRAV
    rot = [
        [1.0 - 2.0 * (qy * qy + qz * qz), 2.0 * (qx * qy - qw * qz), 2.0 * (qx * qz + qw * qy)],
        [2.0 * (qx * qy + qw * qz), 1.0 - 2.0 * (qx * qx + qz * qz), 2.0 * (qy * qz - qw * qx)],
        [2.0 * (qx * qz - qw * qy), 2.0 * (qy * qz + qw * qx), 1.0 - 2.0 * (qx * qx + qy * qy)],
    ]
    tq = f[3:6]
    acc = [
        inert[c] * (rot[0][c] * tq[0] + rot[1][c] * tq[1] + rot[2][c] * tq[2]) for c in range(3)
    ]
    spin = [
        turn[r] + (rot[r][0] * acc[0] + rot[r][1] * acc[1] + rot[r][2] * acc[2]) for r in range(3)
    ]
    sx, sy, sz = spin
    dq = [
        -(sx * qx + sy * qy + sz * qz),
        sx * qw + sy * qz - sz * qy,
        sy * qw + sz * qx - sx * qz,
        sz * qw + sx * qy - sy * qx,
    ]
    scale = lax.rsqrt(1.0 + 0.25 * (sx * sx + sy * sy + sz * sz))
    quat = [(q + 0.5 * k) * scale for q, k in zip((qw, qx, qy, qz), dq)]
    rows = [pos[i] + velo[i] for i in range(3)] + quat + velo + spin
    for i, v in enumerate(rows):
        result[i : i + 1, :] = v
    small = pltpu.make_async_copy(result, b_out, sems.at[1])
    small.start()
    small.wait()
    out.wait()


def shards(sizes, *args):
    pop = args[0]
    span_x, span_z, span_y = pop.shape[1:]
    cells = span_x * span_z
    body_own = args[6].shape[1]
    slots = args[5].shape[-1]
    links = args[1].shape[-1]
    chunks = links // span_y
    owners = sizes[0] * sizes[1]
    devices = 2 * owners
    cap = max(1, 2 * slots // owners)
    m_rows = -(-NM // (slots // cap))
    args = list(args)
    for k in (1, 2, 3):
        args[k] = args[k].reshape(chunks, span_y)
    args[4] = args[4].reshape(3 * chunks, span_y)
    args[5] = args[5].reshape(1, slots)
    args[10] = args[10].reshape(1, -1)
    vm = pl.BlockSpec(memory_space=pltpu.VMEM)
    dma = pltpu.SemaphoreType.DMA
    V = lambda *s: pltpu.VMEM(s, F32)
    VI = lambda *s: pltpu.VMEM(s, I32)
    args = [pltpu.with_memory_space_constraint(v, pltpu.MemorySpace.HBM) for v in args]
    hbm = pl.BlockSpec(memory_space=pltpu.MemorySpace.HBM)
    outs = pl.pallas_call(
        functools.partial(kernel, (sizes[0], sizes[1], cap)),
        out_shape=(
            jax.ShapeDtypeStruct(pop.shape, F32),
            jax.ShapeDtypeStruct((24, body_own), F32),
            jax.ShapeDtypeStruct((devices, m_rows + 1, slots), F32),
            jax.ShapeDtypeStruct((devices, 1, slots), F32),
        ),
        in_specs=[hbm] * len(args),
        out_specs=(vm,) * 4,
        scratch_shapes=[
            *[pltpu.VMEM(v.shape, v.dtype) for v in args],
            V(19, cells, span_y),
            V(2, 5, span_z, span_y), V(2, 5, span_z, span_y),
            V(2, 5, span_x, span_y), V(2, 5, span_x, span_y),
            V(2, 8, span_y), V(2, 8, span_y),
            V(2, 8, cells), V(2, 4, 8, cells),
            V(cells, span_y),
            V(cells, span_y), VI(cells, span_y),
            V(7, SUB, span_y), V(chunks, NM_PAD, span_y), V(chunks, SUB, span_y),
            pltpu.VMEM((owners * cap, links), BF16), pltpu.VMEM((cells, links), BF16),
            V(NM_PAD, owners * cap), V(SUB, owners * cap),
            V(8, body_own), V(owners, 8, body_own),
            V(owners, m_rows + 1, slots), V(devices, m_rows + 1, slots),
            V(owners, 1, slots), V(devices, 1, slots),
            *[dma] * 11,
            dma((POP_CHUNKS,)), dma((11,)),
        ],
        compiler_params=pltpu.CompilerParams(
            collective_id=0, has_side_effects=True, vmem_limit_bytes=K1_VMEM
        ),
        name="lattice_step",
    )(*args)
    return pl.pallas_call(
        functools.partial(finish, cap),
        out_shape=(
            jax.ShapeDtypeStruct(pop.shape, F32),
            jax.ShapeDtypeStruct((13, body_own), F32),
        ),
        in_specs=[vm] * 4,
        out_specs=(hbm, hbm),
        scratch_shapes=[V(13, body_own), dma((2,))],
        compiler_params=pltpu.CompilerParams(vmem_limit_bytes=K2_VMEM),
        name="finish",
    )(*outs)


def solution(mesh):
    sizes = (mesh.shape["gx"], mesh.shape["gy"])
    link = P("gx", "gz", "gy", None)
    body = P(None, ("gx", "gy"))
    return jax.shard_map(
        functools.partial(shards, sizes),
        mesh=mesh,
        in_specs=(
            P(None, "gx", "gz", "gy"), link, link, link, P(None, "gx", "gz", "gy", None), link,
            body, body, body, body, P(("gx", "gy")), body,
        ),
        out_specs=(P(None, "gx", "gz", "gy"), body),
        check_vma=False,
    )
```

time: 21.4 us -> 15.8 us (0.74)
  Pallas kernels: 20.5 us -> 15 us
    pallas_call x2, Pallas kernels: 20.5 us -> 15 us  [the longest x1 13.9 us: shards(): pl.pallas_call(functools.partial(kernel, (sizes[0], sizes[1], cap)), out_...]
where the time goes in v2:
time: 15.8 us; the launch traced here: 15.6 us
  Pallas kernels  15 us (95%)
  between operations  0.64 us (4%)
    pallas_call x1, Pallas kernels, shards(): pl.pallas_call(functools.partial(kernel, (sizes[0], sizes[1], cap)), out_...  13.9 us
    pallas_call x1, Pallas kernels, shards(): pl.pallas_call(functools.partial(finish, cap), out_shape=(jax.ShapeDtypeS...  1.06 us

profile of v2, /device:TPU:0, one launch (start us, length us, event | category | flops | bytes accessed | tf_op | source)
XLA Modules:
  0.0 15.6 jit_solution(12860347525894945107)
XLA Ops:
  0.6 13.9 %lattice_step.1 = (f32[19,8,16,128]{3,2,1,0:T(8,128)S(1)}, f32[24,128]{1,0:T(8,128)S(1)}, f32[32,4,128]{2,1,0:T(4,128)S(1)}, f32[32,1,128]{2,1,0:T(1,128)S(1)}) custom-call(f32[19,8,16,128]{3,2,1,0:T(8,128)} %pop_h.1, s32[8,128]{1,0:T(8,128)} %bitcast.7, s32[8,128]{1,0:T(8,128)} %bitcast.8, s32[8,128]{1,0:T(8,128)} %bitcast.9, f32[24,128]{1,0:T(8,128)} %bitcast.6, ...), custom_call_target="tpu_custom_call" | custom-call | tf_op jit(solution)/shard_map/lattice_step/pallas_call | solution.py:573
  14.6 1.1 %finish.1 = (f32[19,8,16,128]{3,2,1,0:T(8,128)}, f32[13,128]{1,0:T(8,128)}) custom-call(f32[19,8,16,128]{3,2,1,0:T(8,128)S(1)} %get-tuple-element.6.nxt, f32[24,128]{1,0:T(8,128)S(1)} %get-tuple-element.7.state, f32[32,4,128]{2,1,0:T(4,128)S(1)} %get-tuple-element.8.got_m, f32[32,1,128]{2,1,0:T(1,128)S(1)} %get-tuple-element.9.got_a), custom_call_target="tpu_custom_call" | custom-call | tf_op jit(solution)/shard_map/finish/pallas_call | solution.py:606

commit v3 on v2

--- a/solution.py
+++ b/solution.py
@@ -17,6 +17,7 @@
 OPP = [0, 2, 1, 4, 3, 6, 5, 8, 7, 10, 9, 12, 11, 14, 13, 16, 15, 18, 17]
 OMEGA = 1.25
 POP_CHUNKS = 4
+OUT_CHUNKS = 4
 K1_VMEM = 24 * 1024 * 1024
 K2_VMEM = 4 * 1024 * 1024
 GRAV = 0.02
@@ -67,7 +68,7 @@
     sizes,
     pop_h, *rest,
 ):
-    small_h, outs, rest = rest[:11], rest[11:15], rest[15:]
+    small_h, outs, rest = rest[:11], rest[11:18], rest[18:]
     pop, small, rest = rest[0], rest[1:12], rest[12:]
     step(sizes, pop_h, small_h, pop, *small, *outs, *rest)
 
@@ -75,9 +76,9 @@
 def step(
     sizes, pop_h, small_h,
     pop, lcell, ldir, lslot, larm, bb_ref, bpos, bquat, bvel, bspin, imass, iinert,
-    nxt, state, got_m, got_a,
-    relaxed, sendx, xin, sendz, zin, sende, ein, sendy, yin, ycols,
-    post_map, dmap, links_f, comps_m, comps_a, place_hot, row_hot, slot_m, slot_a,
+    nxt, post_map, dmap, ycols, state, got_m, got_a,
+    relaxed, sendx, xin, sendz, zin, sende, ein, sendy, yin,
+    links_f, comps_m, comps_a, place_hot, row_hot, slot_m, slot_a,
     motion_own, motion_all, send_m, recv_m, send_a, recv_a,
     hs, xr, er, yr, zr, ms, mr, rs, rr, fs, fr, ps, ss,
 ):
@@ -329,18 +330,21 @@
 
     pl.semaphore_wait(barrier, devices - 1)
 
+    remote(sendz, zin, hs, zr, dev(a, b, oe)).start()
     for s in range(2):
         xt, yt = (ap, bp) if s == 0 else (am, bm)
         for k, t in enumerate((dev(a, yt, e), dev(ap, yt, e), dev(am, yt, e), dev(a, yt, oe))):
             remote(sendy.at[s], yin.at[s, k], hs, yr, t).start()
+
+    def send_motion(o):
+        remote(motion_own, motion_all.at[me], ms, mr, peer_of(o, e)[1]).start()
+
+    loop(1, owners, send_motion)
+
+    for s in range(2):
+        xt, yt = (ap, bp) if s == 0 else (am, bm)
         remote(sendx.at[s], xin.at[s], hs, xr, dev(xt, b, e)).start()
         remote(sende.at[s], ein.at[s], hs, er, dev(xt, b, oe)).start()
-    remote(sendz, zin, hs, zr, dev(a, b, oe)).start()
-
-    def send_motion(o):
-        remote(motion_own, motion_all.at[me], ms, mr, peer_of(o, e)[1]).start()
-
-    loop(1, owners, send_motion)
 
     def send_response(o):
         for z in (e, oe):
@@ -371,12 +375,9 @@
 
     for k in (5, 6, 9, 10):
         small_in[k].wait()
-    wait_bytes(xin, xr)
-    wait_bytes(ein, er)
     wait_bytes(zin, zr)
     iz = lax.broadcasted_iota(I32, (span_z, span_y), 0)
-    iy = lax.broadcasted_iota(I32, (span_z, span_y), 1)
-    for x in range(span_x):
+    def streamed(x):
         for i in range(19):
             cx, cy, cz = VEL[i]
             sx = x - cx
@@ -399,6 +400,9 @@
             if cy:
                 v = pltpu.roll(v, 1 if cy > 0 else span_y - 1, 1)
             nxt[i, x] = v
+
+    for x in range(1, span_x - 1):
+        streamed(x)
 
     state[0:16, :] = jnp.concatenate(
         [bpos[...], bquat[...], bvel[...], bspin[...], iinert[...]], 0
@@ -453,10 +457,37 @@
     both.append(jnp.zeros((span_y - 16, cells), F32))
     ycols[...] = jnp.concatenate(both, 0).T
 
+    wait_bytes(xin, xr)
+    wait_bytes(ein, er)
+    streamed(0)
+    streamed(span_x - 1)
+
+    wait_bytes(sendx, hs)
+    wait_bytes(sende, hs)
+    wait_bytes(yin, hs)
+    wait_bytes(sendz, hs)
+    wait_bytes(motion_all.at[pl.ds(0, owners - 1)], ms)
+    wait_bytes(recv_m.at[pl.ds(0, devices - 1)], rs)
+    wait_bytes(recv_a.at[pl.ds(0, devices - 1)], fs)
+
+    wait_bytes(recv_m.at[pl.ds(0, devices - 1)], rr)
+    wait_bytes(recv_a.at[pl.ds(0, devices - 1)], fr)
+    got_m[...] = recv_m[...]
+    got_a[...] = recv_a[...]
+
+
+def finish(
+    cap, nxt, bounce_map, dmap, ycols, state, got_m, got_a, a_out, b_out, done, result, sems
+):
+    span_x, span_z, span_y = nxt.shape[1:]
+    iy = lax.broadcasted_iota(I32, (span_z, span_y), 1)
+    out = [pltpu.make_async_copy(nxt.at[0], a_out.at[0], sems.at[1])]
+    out[0].start()
+    chunk = span_x // OUT_CHUNKS
     for x in range(span_x):
         rows = slice(x * span_z, (x + 1) * span_z)
         at = dmap[rows, :]
-        bounce = post_map[rows, :]
+        bounce = bounce_map[rows, :]
         for i in range(1, 19):
             cy = VEL[i][1]
             v = nxt[i, x]
@@ -464,25 +495,14 @@
                 s = 0 if cy > 0 else 1
                 j = 8 * s + YD[s].index(i)
                 v = jnp.where(iy == (0 if cy > 0 else span_y - 1), ycols[rows, j : j + 1], v)
-            nxt[i, x] = jnp.where(at == OPP[i], bounce, v)
-
-    wait_bytes(sendx, hs)
-    wait_bytes(sende, hs)
-    wait_bytes(yin, hs)
-    wait_bytes(sendz, hs)
-    wait_bytes(motion_all.at[pl.ds(0, owners - 1)], ms)
-    wait_bytes(recv_m.at[pl.ds(0, devices - 1)], rs)
-    wait_bytes(recv_a.at[pl.ds(0, devices - 1)], fs)
-
-    wait_bytes(recv_m.at[pl.ds(0, devices - 1)], rr)
-    wait_bytes(recv_a.at[pl.ds(0, devices - 1)], fr)
-    got_m[...] = recv_m[...]
-    got_a[...] = recv_a[...]
-
-
-def finish(cap, nxt, state, got_m, got_a, a_out, b_out, result, sems):
-    out = pltpu.make_async_copy(nxt, a_out, sems.at[0])
-    out.start()
+            done[i - 1, x] = jnp.where(at == OPP[i], bounce, v)
+        if x % chunk == chunk - 1:
+            part = pl.ds(x + 1 - chunk, chunk)
+            c = pltpu.make_async_copy(
+                done.at[:, part], a_out.at[pl.ds(1, 18), part], sems.at[2 + x // chunk]
+            )
+            c.start()
+            out.append(c)
     devices, slots = got_a.shape[0], got_a.shape[2]
     per_row = slots // cap
     m_rows = got_m.shape[1] - 1
@@ -540,10 +560,11 @@
     rows = [pos[i] + velo[i] for i in range(3)] + quat + velo + spin
     for i, v in enumerate(rows):
         result[i : i + 1, :] = v
-    small = pltpu.make_async_copy(result, b_out, sems.at[1])
+    small = pltpu.make_async_copy(result, b_out, sems.at[0])
     small.start()
+    for c in out:
+        c.wait()
     small.wait()
-    out.wait()
 
 
 def shards(sizes, *args):
@@ -567,19 +588,21 @@
     vm = pl.BlockSpec(memory_space=pltpu.VMEM)
     dma = pltpu.SemaphoreType.DMA
     V = lambda *s: pltpu.VMEM(s, F32)
-    VI = lambda *s: pltpu.VMEM(s, I32)
     args = [pltpu.with_memory_space_constraint(v, pltpu.MemorySpace.HBM) for v in args]
     hbm = pl.BlockSpec(memory_space=pltpu.MemorySpace.HBM)
     outs = pl.pallas_call(
         functools.partial(kernel, (sizes[0], sizes[1], cap)),
         out_shape=(
             jax.ShapeDtypeStruct(pop.shape, F32),
+            jax.ShapeDtypeStruct((cells, span_y), F32),
+            jax.ShapeDtypeStruct((cells, span_y), I32),
+            jax.ShapeDtypeStruct((cells, span_y), F32),
             jax.ShapeDtypeStruct((24, body_own), F32),
             jax.ShapeDtypeStruct((devices, m_rows + 1, slots), F32),
             jax.ShapeDtypeStruct((devices, 1, slots), F32),
         ),
         in_specs=[hbm] * len(args),
-        out_specs=(vm,) * 4,
+        out_specs=(vm,) * 7,
         scratch_shapes=[
             *[pltpu.VMEM(v.shape, v.dtype) for v in args],
             V(19, cells, span_y),
@@ -587,8 +610,6 @@
             V(2, 5, span_x, span_y), V(2, 5, span_x, span_y),
             V(2, 8, span_y), V(2, 8, span_y),
             V(2, 8, cells), V(2, 4, 8, cells),
-            V(cells, span_y),
-            V(cells, span_y), VI(cells, span_y),
             V(7, SUB, span_y), V(chunks, NM_PAD, span_y), V(chunks, SUB, span_y),
             pltpu.VMEM((owners * cap, links), BF16), pltpu.VMEM((cells, links), BF16),
             V(NM_PAD, owners * cap), V(SUB, owners * cap),
@@ -609,9 +630,9 @@
             jax.ShapeDtypeStruct(pop.shape, F32),
             jax.ShapeDtypeStruct((13, body_own), F32),
         ),
-        in_specs=[vm] * 4,
+        in_specs=[vm] * 7,
         out_specs=(hbm, hbm),
-        scratch_shapes=[V(13, body_own), dma((2,))],
+        scratch_shapes=[V(18, *pop.shape[1:]), V(13, body_own), dma((2 + OUT_CHUNKS,))],
         compiler_params=pltpu.CompilerParams(vmem_limit_bytes=K2_VMEM),
         name="finish",
     )(*outs)

time: 15.8 us -> 15.3 us (0.968)
  Pallas kernels: 15 us -> 14.5 us
    pallas_call x1, Pallas kernels: 13.9 us -> 13.2 us  [shards(): pl.pallas_call(functools.partial(kernel, (sizes[0], sizes[1], cap)), out_...]
    pallas_call x1, Pallas kernels: 1.06 us -> 1.31 us  [shards(): pl.pallas_call(functools.partial(finish, cap), out_shape=(jax.ShapeDtypeS...]
where the time goes in v3:
time: 15.3 us; the launch traced here: 15.2 us
  Pallas kernels  14.5 us (95%)
  between operations  0.64 us (4%)
    pallas_call x1, Pallas kernels, shards(): pl.pallas_call(functools.partial(kernel, (sizes[0], sizes[1], cap)), out_...  13.2 us
    pallas_call x1, Pallas kernels, shards(): pl.pallas_call(functools.partial(finish, cap), out_shape=(jax.ShapeDtypeS...  1.31 us

profile of v3, /device:TPU:0, one launch (start us, length us, event | category | flops | bytes accessed | tf_op | source)
XLA Modules:
  0.0 15.2 jit_solution(7696392897678339358)
XLA Ops:
  0.6 13.2 %lattice_step.1 = (f32[19,8,16,128]{3,2,1,0:T(8,128)S(1)}, f32[128,128]{1,0:T(8,128)S(1)}, s32[128,128]{1,0:T(8,128)S(1)}, f32[128,128]{1,0:T(8,128)S(1)}, f32[2...) custom-call(f32[19,8,16,128]{3,2,1,0:T(8,128)} %pop_h.1, s32[8,128]{1,0:T(8,128)} %bitcast.7, ...), custom_call_target="tpu_custom_call" | custom-call | tf_op jit(solution)/shard_map/lattice_step/pallas_call | solution.py:593
  13.9 1.3 %finish.1 = (f32[19,8,16,128]{3,2,1,0:T(8,128)}, f32[13,128]{1,0:T(8,128)}) custom-call(f32[19,8,16,128]{3,2,1,0:T(8,128)S(1)} %get-tuple-element.9.nxt, f32[128,128]{1,0:T(8,128)S(1)} %get-tuple-element.10.bounce_map, s32[128,128]{1,0:T(8,128)S(1)} %get-tuple-element.11.dmap, f32[128,128]{1,0:T(8,128)S(1)} %get-tuple-element.12.ycols, ...), custom_call_target="tpu_custom_call" | custom-call | tf_op jit(solution)/shard_map/finish/pallas_call | solution.py:627

commit v4 on v3

--- a/solution.py
+++ b/solution.py
@@ -346,14 +346,6 @@
         remote(sendx.at[s], xin.at[s], hs, xr, dev(xt, b, e)).start()
         remote(sende.at[s], ein.at[s], hs, er, dev(xt, b, oe)).start()
 
-    def send_response(o):
-        for z in (e, oe):
-            p, target = peer_of(o, z)
-            remote(send_m.at[p], recv_m.at[own], rs, rr, target).start()
-
-    loop(1, owners, send_response)
-    remote(send_m.at[me], recv_m.at[own], rs, rr, dev(a, b, oe)).start()
-
     parts = [jnp.zeros(tile, F32) for _ in range(4)]
     for r in range(cells):
         got = pick(spread(post_map[r : r + 1, :], parts[0]), lane_of)
@@ -372,6 +364,14 @@
 
     loop(1, owners, send_push)
     remote(send_a.at[me], recv_a.at[own], fs, fr, dev(a, b, oe)).start()
+
+    def send_response(o):
+        for z in (e, oe):
+            p, target = peer_of(o, z)
+            remote(send_m.at[p], recv_m.at[own], rs, rr, target).start()
+
+    loop(1, owners, send_response)
+    remote(send_m.at[me], recv_m.at[own], rs, rr, dev(a, b, oe)).start()
 
     for k in (5, 6, 9, 10):
         small_in[k].wait()

time: 15.3 us -> 15 us (0.980)
  Pallas kernels: 14.5 us -> 14.2 us
    pallas_call x1, Pallas kernels: 13.2 us -> 12.9 us  [shards(): pl.pallas_call(functools.partial(kernel, (sizes[0], sizes[1], cap)), out_...]
where the time goes in v4:
time: 15 us; the launch traced here: 14.9 us
  Pallas kernels  14.2 us (95%)
  between operations  0.64 us (4%)
    pallas_call x1, Pallas kernels, shards(): pl.pallas_call(functools.partial(kernel, (sizes[0], sizes[1], cap)), out_...  12.9 us
    pallas_call x1, Pallas kernels, shards(): pl.pallas_call(functools.partial(finish, cap), out_shape=(jax.ShapeDtypeS...  1.31 us

profile of v4, /device:TPU:0, one launch (start us, length us, event | category | flops | bytes accessed | tf_op | source)
XLA Modules:
  0.0 14.9 jit_solution(7188844641547911369)
XLA Ops:
  0.6 12.9 %lattice_step.1 = (f32[19,8,16,128]{3,2,1,0:T(8,128)S(1)}, f32[128,128]{1,0:T(8,128)S(1)}, s32[128,128]{1,0:T(8,128)S(1)}, f32[128,128]{1,0:T(8,128)S(1)}, f32[2...) custom-call(f32[19,8,16,128]{3,2,1,0:T(8,128)} %pop_h.1, s32[8,128]{1,0:T(8,128)} %bitcast.7, ...), custom_call_target="tpu_custom_call" | custom-call | tf_op jit(solution)/shard_map/lattice_step/pallas_call | solution.py:593
  13.5 1.3 %finish.1 = (f32[19,8,16,128]{3,2,1,0:T(8,128)}, f32[13,128]{1,0:T(8,128)}) custom-call(f32[19,8,16,128]{3,2,1,0:T(8,128)S(1)} %get-tuple-element.9.nxt, f32[128,128]{1,0:T(8,128)S(1)} %get-tuple-element.10.bounce_map, s32[128,128]{1,0:T(8,128)S(1)} %get-tuple-element.11.dmap, f32[128,128]{1,0:T(8,128)S(1)} %get-tuple-element.12.ycols, ...), custom_call_target="tpu_custom_call" | custom-call | tf_op jit(solution)/shard_map/finish/pallas_call | solution.py:627
